TPU v7x, 32 devices: a whole 2x2x4 slice. The times are simulated.
32 devices in a mesh: guide: 2 (over core), tensor: 2 (over y), batch: 8 (over z, x).
Axes of the slice: x: 2, y: 2, z: 4, core: 2. Of those that a mesh axis runs over, the one named last changes fastest.
Arguments:
- latents: float32 [8, 16, 448], P('batch'), may hold values from -6 to 6
- lengths: int32 [8], P('batch'), may hold values from 1 to 448, 2240 in all
- timesteps: int32 [8], P('batch'), may hold values from 100 to 599
- guidance: float32 [8], P('batch'), may hold values from 1.5 to 6
- condition: float32 [2, 8, 1152], P('guide', 'batch'), may hold values from -6 to 6
- embed_weight: float32 [16, 1152], replicated, may hold values from -1.5 to 1.5
- modulation_weight: bfloat16 [2, 1152, 6, 1152], P(None, 'batch', None, 'tensor'), may hold values from -0.1875 to 0.1875
- final_modulation: bfloat16 [1152, 2, 1152], P('batch', None, 'tensor'), may hold values from -0.1875 to 0.1875
- qkv_weight: bfloat16 [2, 1152, 3, 1152], P(None, 'batch', None, 'tensor'), may hold values from -15 to 15
- proj_weight: bfloat16 [2, 1152, 1152], P(None, 'tensor', 'batch'), may hold values from -0.1875 to 0.1875
- up_weight: bfloat16 [2, 1152, 4608], P(None, 'batch', 'tensor'), may hold values from -0.1875 to 0.1875
- down_weight: bfloat16 [2, 4608, 1152], P(None, 'tensor', 'batch'), may hold values from -0.09375 to 0.09375
- output_weight: bfloat16 [1152, 16], replicated, may hold values from -0.1875 to 0.1875
Outputs:
- guided_noise: float32 [8, 16, 448], P('batch', 'guide', 'tensor')
- previous_latents: float32 [8, 16, 448], P('batch', 'guide', 'tensor')
Inputs may be any that keep to these rules, and one draw needn't show every extreme that they name: `lengths`: at least one request has exactly 448 live tokens; all requests together have 8 * 448 * 5 // 8.
All inputs are finite; a program needn't handle non-finite values. No bound on the sum of `lengths` on one device may be relied on, other than what follows from the above.
Results may differ from a plain program's by a relative error of at most 0.025.
Values may be sent and summed in bfloat16 or wider, within the bound.
No kernel may reach another device: no remote copies, remote signals or barrier semaphores. Data moves between devices by JAX's collectives and lax.ppermute only.
A program may use at most 128 MiB of HBM per device.

v0:
```python
import math
import jax
import jax.numpy as jnp
from jax import lax
from jax.sharding import PartitionSpec as P

HDIM = 72
TRAIN_STEPS = 1000
STRIDE = 20
norm_epsilon = 1e-06


def from_partner(block, axis, distance):
    count = lax.axis_size(axis)
    route = []
    for low in range(count):
        high = low | 1 << distance
        if high != low and high < count:
            route += [(low, high), (high, low)]
    return lax.ppermute(block, axis, route)


def layer_norm(values):
    center = values - jnp.mean(values, axis=-1, keepdims=True)
    spread = jnp.mean(center * center, axis=-1, keepdims=True)
    return center * lax.rsqrt(spread + norm_epsilon)


def modulate(values, shift, scale):
    return layer_norm(values) * (1.0 + scale[:, None, :]) + shift[:, None, :]


def position_table(row_count, width):
    rows_at = jnp.arange(row_count, dtype=jnp.int32).astype(jnp.float32)
    half_width = width // 2
    frequency = jnp.exp(
        jnp.arange(half_width, dtype=jnp.float32) * (-math.log(10000.0) / half_width)
    )
    angles = rows_at[:, None] * frequency[None, :]
    return jnp.concatenate([jnp.sin(angles), jnp.cos(angles)], axis=1)


def attend(operands):
    projected_item, key_live = operands
    score_scale = 1.0 / math.sqrt(HDIM)
    scores = (
        jnp.einsum(
            "qhd,khd->hqk",
            projected_item[:, 0],
            projected_item[:, 1],
            preferred_element_type=jnp.float32,
        )
        * score_scale
    )
    scores = jnp.where(key_live[None, None, :], scores, -jnp.inf)
    row_max = jnp.max(scores, axis=-1, keepdims=True)
    exp_scores = jnp.exp(scores - row_max)
    probabilities = (exp_scores / jnp.sum(exp_scores, axis=-1, keepdims=True)).astype(jnp.bfloat16)
    attended = jnp.einsum(
        "hqk,khd->qhd", probabilities, projected_item[:, 2], preferred_element_type=jnp.float32
    )
    return attended.astype(jnp.bfloat16).reshape(
        attended.shape[0], attended.shape[1] * attended.shape[2]
    )


def local(
    latents,
    lengths,
    timesteps,
    guidance,
    condition,
    embed_weight,
    modulation_weight,
    final_modulation,
    qkv_weight,
    proj_weight,
    up_weight,
    down_weight,
    output_weight,
):
    tensor_count = lax.axis_size("tensor")
    batch_count = lax.axis_size("batch")
    tensor_at = lax.axis_index("tensor")
    batch_at = lax.axis_index("batch")
    guide_at = lax.axis_index("guide")
    req_local, patch_size, max_len = latents.shape
    width = embed_weight.shape[1]
    layer_count = qkv_weight.shape[0]
    head_cols = qkv_weight.shape[3]
    heads_local = head_cols // HDIM
    rows_local = max_len // tensor_count
    width_piece = width // batch_count
    mod_count = 6 * layer_count + 2
    is_first = guide_at == 0

    def rows_product(activation, shard):
        return jnp.dot(
            activation,
            lax.all_gather(shard, "batch", axis=0, tiled=True),
            preferred_element_type=jnp.float32,
        )

    def cols_product(activation, shard):
        return jnp.dot(
            activation,
            lax.all_gather(shard, "batch", axis=1, tiled=True),
            preferred_element_type=jnp.float32,
        )

    cond_act = jax.nn.silu(condition[0]).astype(jnp.bfloat16)
    cond_all = lax.all_gather(cond_act, "batch", axis=0, tiled=True)
    cond_cols = lax.dynamic_slice_in_dim(cond_all, batch_at * width_piece, width_piece, 1)
    block_local = jnp.transpose(modulation_weight, (1, 0, 2, 3)).reshape(
        width_piece, 6 * layer_count * head_cols
    )
    mod_local = jnp.concatenate(
        [block_local, final_modulation.reshape(width_piece, 2 * head_cols)], axis=1
    )
    mod_mine = lax.psum_scatter(
        jnp.dot(cond_cols, mod_local, preferred_element_type=jnp.float32),
        "batch",
        scatter_dimension=0,
        tiled=True,
    )
    mod_full = lax.all_gather(
        mod_mine.reshape(req_local, mod_count, head_cols), "tensor", axis=2, tiled=True
    )
    positions = jnp.arange(max_len, dtype=jnp.int32)
    live_mask = positions[None, :] < lengths[:, None]
    own_start = tensor_at * rows_local
    own_latents = lax.dynamic_slice_in_dim(latents, own_start, rows_local, 2)
    own_live = lax.dynamic_slice_in_dim(live_mask, own_start, rows_local, 1)
    hidden_state = (
        jnp.einsum("rpl,pd->rld", latents, embed_weight, precision=lax.Precision.HIGHEST)
        + position_table(max_len, width)[None]
    )
    for layer_at in range(layer_count):
        modulation = mod_full[:, 6 * layer_at : 6 * layer_at + 6]
        normed = modulate(hidden_state, modulation[:, 0], modulation[:, 1]).astype(jnp.bfloat16)
        projected = rows_product(
            normed.reshape(req_local * max_len, width),
            qkv_weight[layer_at].reshape(width_piece, 3 * head_cols),
        ).astype(jnp.bfloat16)
        projected = projected.reshape(req_local, max_len, 3, heads_local, HDIM)
        attended = lax.map(attend, (projected, live_mask))
        branch = cols_product(
            attended.reshape(req_local * max_len, head_cols), proj_weight[layer_at]
        ).reshape(req_local, max_len, width)
        branch = lax.psum(branch.astype(jnp.bfloat16), "tensor").astype(jnp.float32)
        hidden_state = hidden_state + modulation[:, 2][:, None, :] * branch
        normed = modulate(hidden_state, modulation[:, 3], modulation[:, 4]).astype(jnp.bfloat16)
        hidden_units = jax.nn.gelu(
            rows_product(normed.reshape(req_local * max_len, width), up_weight[layer_at]),
            approximate=True,
        ).astype(jnp.bfloat16)
        branch = cols_product(hidden_units, down_weight[layer_at]).reshape(
            req_local, max_len, width
        )
        branch = lax.psum(branch.astype(jnp.bfloat16), "tensor").astype(jnp.float32)
        hidden_state = hidden_state + modulation[:, 5][:, None, :] * branch
    hidden_state = lax.dynamic_slice_in_dim(hidden_state, own_start, rows_local, 1)
    final_in = modulate(
        hidden_state, mod_full[:, 6 * layer_count], mod_full[:, 6 * layer_count + 1]
    ).astype(jnp.bfloat16)
    noise_own = jnp.einsum(
        "rld,dp->rpl", final_in, output_weight, preferred_element_type=jnp.float32
    )
    half_patch = patch_size // 2
    mine_noise = lax.dynamic_slice_in_dim(noise_own, guide_at * half_patch, half_patch, 1)
    other_noise = lax.dynamic_slice_in_dim(noise_own, (1 - guide_at) * half_patch, half_patch, 1)
    partner_noise = from_partner(other_noise, "guide", 0)
    cond_noise = jnp.where(is_first, mine_noise, partner_noise)
    uncond_noise = jnp.where(is_first, partner_noise, mine_noise)
    live_out = own_live[:, None, :]
    guided = uncond_noise + guidance[:, None, None] * (cond_noise - uncond_noise)
    guided = jnp.where(live_out, guided, 0.0)
    half_latents = lax.dynamic_slice_in_dim(own_latents, guide_at * half_patch, half_patch, 1)
    beta_values = jnp.linspace(0.0001, 0.02, TRAIN_STEPS, dtype=jnp.float32)
    alpha_bar = jnp.cumprod(1.0 - beta_values)
    step_ids = jnp.arange(TRAIN_STEPS, dtype=jnp.int32)
    alpha_now = jnp.sum(
        jnp.where(step_ids[None, :] == timesteps[:, None], alpha_bar[None, :], 0.0), axis=1
    )[:, None, None]
    alpha_prev = jnp.sum(
        jnp.where(step_ids[None, :] == (timesteps - STRIDE)[:, None], alpha_bar[None, :], 0.0),
        axis=1,
    )[:, None, None]
    start_est = (half_latents - jnp.sqrt(1.0 - alpha_now) * guided) / jnp.sqrt(alpha_now)
    previous = jnp.sqrt(alpha_prev) * start_est + jnp.sqrt(1.0 - alpha_prev) * guided
    previous = jnp.where(live_out, previous, 0.0)
    return (guided, previous)


def solution(mesh):
    in_specs = (
        P("batch", None, None),
        P("batch"),
        P("batch"),
        P("batch"),
        P("guide", "batch", None),
        P(),
        P(None, "batch", None, "tensor"),
        P("batch", None, "tensor"),
        P(None, "batch", None, "tensor"),
        P(None, "tensor", "batch"),
        P(None, "batch", "tensor"),
        P(None, "tensor", "batch"),
        P(),
    )
    out_specs = (P("batch", "guide", "tensor"), P("batch", "guide", "tensor"))
    return jax.shard_map(local, mesh=mesh, in_specs=in_specs, out_specs=out_specs, check_vma=False)
```

profile of v0, /device:TPU:1, one launch (start us, length us, event | category | flops | bytes accessed | tf_op | source)
XLA Modules:
  0.0 909.3 jit_solution(10363798787262294825)
XLA Ops:
  7.2 0.7 fusion.119
  7.9 25.4 %all-gather.6 = bf16[8,1,1152]{2,1,0:T(2,128)(2,1)S(1)} all-gather(bf16[1,1,1152]{2,1,0:T(2,128)(2,1)S(1)} %fusion.119), channel_id=1, replica_groups=mesh['guide'=2,'tensor'=2,'batch'=8] {'batch'}, dimensions={0}, use_global_device_ids=true | all-gather | bytes 20736 | tf_op jit(solution)/shard_map/all_gather | solution.py:112
  33.3 2.2 copy.40
  35.6 3.2 reshape.338
  39.2 2.7 fusion.58
  42.3 1.3 reshape_squeeze.6
  43.8 0.8 fusion.144
  44.6 4.1 multiply_sine_fusion
  48.7 2.1 fusion.145
  52.5 64.8 %all-reduce.16.cloned.1.call-done = f32[8,8064]{1,0:T(8,128)} async-done(((f32[8,8064]{1,0:T(8,128)}), f32[8,8064]{1,0:T(8,128)}) %all-reduce.16.cloned.1.call-update) | async-done | bytes 258064
  117.3 1.7 dynamic-slice_reduce_fusion
  119.2 6.8 all_gather.31
  126.0 62.0 %slice_reduce_fusion.2 = (f32[1152]{0:T(1024)S(1)}, f32[1152]{0:T(1024)S(1)}, f32[1152]{0:T(1024)S(1)}, f32[1152]{0:T(1024)S(1)}, f32[1152]{0:T(1024)S(1)}, /*in...) fusion(f32[1,14,1152]{1,0,2:T(1,128)S(1)} %all_gather.31), kind=kLoop, calls=%fused_computation.104 | loop fusion | flops 5760 | bytes 129024 | tf_op jit(solution)/shard_map/slice | solution.py:161
  188.0 4.9 all-gather.16.cloned.1.call-done
  192.9 5.8 convolution_convert_fusion.1
  198.7 3.0 copy.43
  201.7 5.9 fusion.146
  207.6 3.9 fusion.65
  211.5 26.3 %all-gather.20.cloned.1.call-done = bf16[1,576,1152]{1,2,0:T(8,128)(2,1)} async-done(((bf16[1,576,144]{1,2,0:T(8,128)(2,1)}), bf16[1,576,1152]{1,2,0:T(8,128)(2,1)}) %all-gather.20.cloned.1.call-update) | async-done | bytes 1327120 | tf_op jit(solution)/shard_map/all_gather | solution.py:107
  237.8 3.5 fusion.50
  241.4 1.2 fusion.141
  243.1 1.2 fusion.142
  244.3 35.8 %all-reduce.8.cloned.1.call-done = bf16[1,448,1152]{2,1,0:T(8,128)(2,1)} async-done(((bf16[1,448,1152]{2,1,0:T(8,128)(2,1)}), bf16[1,448,1152]{2,1,0:T(8,128)(2,1)}) %all-reduce.8.cloned.1.call-update) | async-done | bytes 1032208 | tf_op jit(solution)/shard_map/psum | solution.py:150
  280.1 2.2 fusion.140
  282.8 85.9 %all-gather.22.cloned.1.call-done = bf16[1,1152,2304]{2,1,0:T(8,128)(2,1)} async-done(((bf16[1,144,2304]{2,1,0:T(8,128)(2,1)}), bf16[1,1152,2304]{2,1,0:T(8,128)(2,1)}) %all-gather.22.cloned.1.call-update) | async-done | bytes 5308432 | tf_op jit(solution)/shard_map/all_gather | solution.py:100
  368.6 87.5 %all-gather.24.cloned.1.call-done = bf16[1,2304,1152]{1,2,0:T(8,128)(2,1)} async-done(((bf16[1,2304,144]{1,2,0:T(8,128)(2,1)}), bf16[1,2304,1152]{1,2,0:T(8,128)(2,1)}) %all-gather.24.cloned.1.call-update) | async-done | bytes 5308432 | tf_op jit(solution)/shard_map/all_gather | solution.py:107
  456.2 10.9 %fusion.55 = bf16[1,448,1152]{2,1,0:T(8,128)(2,1)} fusion(bf16[1,2304,1152]{1,2,0:T(8,128)(2,1)} %all-gather.24.cloned.1.call-done, bf16[1,1152,2304]{2,1,0:T(8,128)(2,1)} %all-gather.22.cloned.1.call-done, f32[1,448,1152]{2,1,0:T(8,128)S(1)} %get-tuple-element.47, f32[1152]{0:T(1024)S(1)} %get-tuple-element.34, f32[1152]{0:T(1024)S(1)} %get-tuple-element.35, ...), kind=kOutput, calls=%fused_computation.54 | convolution fusion | flops 4768727040 | bytes 13726208 | tf_op jit(solution)/shard_map/dot_general | solution.py:105
  467.5 1.2 reshape_squeeze.7
  469.7 36.3 %all-reduce.10.cloned.1.call-done = bf16[1,448,1152]{2,1,0:T(8,128)(2,1)} async-done(((bf16[1,448,1152]{2,1,0:T(8,128)(2,1)}), bf16[1,448,1152]{2,1,0:T(8,128)(2,1)}) %all-reduce.10.cloned.1.call-update) | async-done | bytes 1032208 | tf_op jit(solution)/shard_map/psum | solution.py:160
  506.0 1.7 fusion.137
  508.2 71.6 %all-gather.18.cloned.1.call-done = bf16[1152,1728]{1,0:T(8,128)(2,1)} async-done(((bf16[144,1728]{1,0:T(8,128)(2,1)}), bf16[1152,1728]{1,0:T(8,128)(2,1)}) %all-gather.18.cloned.1.call-update) | async-done | bytes 3981328 | tf_op jit(solution)/shard_map/all_gather | solution.py:100
  579.8 6.0 convolution_convert_fusion
  585.8 3.7 copy.46
  589.5 7.2 fusion.147
  596.7 4.9 fusion.64
  601.6 23.1 %all-gather.26.cloned.1.call-done = bf16[1,576,1152]{1,2,0:T(8,128)(2,1)} async-done(((bf16[1,576,144]{1,2,0:T(8,128)(2,1)}), bf16[1,576,1152]{1,2,0:T(8,128)(2,1)}) %all-gather.26.cloned.1.call-update) | async-done | bytes 1327120 | tf_op jit(solution)/shard_map/all_gather | solution.py:107
  624.7 3.6 fusion.51
  629.9 37.2 %all-reduce.12.cloned.1.call-done = bf16[1,448,1152]{2,1,0:T(8,128)(2,1)} async-done(((bf16[1,448,1152]{2,1,0:T(8,128)(2,1)}), bf16[1,448,1152]{2,1,0:T(8,128)(2,1)}) %all-reduce.12.cloned.1.call-update) | async-done | bytes 1032208 | tf_op jit(solution)/shard_map/psum | solution.py:150
  667.1 1.8 fusion.139
  669.0 1.3 copy-done.3
  670.6 85.2 %all-gather.28.cloned.1.call-done = bf16[1,1152,2304]{2,1,0:T(8,128)(2,1)} async-done(((bf16[1,144,2304]{2,1,0:T(8,128)(2,1)}), bf16[1,1152,2304]{2,1,0:T(8,128)(2,1)}) %all-gather.28.cloned.1.call-update) | async-done | bytes 5308432 | tf_op jit(solution)/shard_map/all_gather | solution.py:100
  755.8 87.5 %all-gather.30.cloned.1.call-done = bf16[1,2304,1152]{1,2,0:T(8,128)(2,1)} async-done(((bf16[1,2304,144]{1,2,0:T(8,128)(2,1)}), bf16[1,2304,1152]{1,2,0:T(8,128)(2,1)}) %all-gather.30.cloned.1.call-update) | async-done | bytes 5308432 | tf_op jit(solution)/shard_map/all_gather | solution.py:107
  843.4 11.6 %fusion.52 = bf16[1,448,1152]{2,1,0:T(8,128)(2,1)} fusion(bf16[1,2304,1152]{1,2,0:T(8,128)(2,1)} %all-gather.30.cloned.1.call-done, bf16[1,1152,2304]{2,1,0:T(8,128)(2,1)} %all-gather.28.cloned.1.call-done, f32[1,448,1152]{2,1,0:T(8,128)} %copy-done.3, f32[1152]{0:T(1024)S(1)} %get-tuple-element.25, f32[1152]{0:T(1024)S(1)} %get-tuple-element.26, ...), kind=kOutput, calls=%fused_computation.53 | convolution fusion | flops 4768727040 | bytes 13726208 | tf_op jit(solution)/shard_map/dot_general | solution.py:105
  856.4 37.5 %all-reduce.14.cloned.1.call-done = bf16[1,448,1152]{2,1,0:T(8,128)(2,1)} async-done(((bf16[1,448,1152]{2,1,0:T(8,128)(2,1)}), bf16[1,448,1152]{2,1,0:T(8,128)(2,1)}) %all-reduce.14.cloned.1.call-update) | async-done | bytes 1032208 | tf_op jit(solution)/shard_map/psum | solution.py:160
  893.9 1.4 fusion.111
  895.3 1.4 multiply_reduce_fusion.4
  897.0 0.8 collective-permute-start
  901.8 0.7 add_select_fusion
  (93 shorter events, 8.8 us)
Async XLA Ops:
  7.2 41.5 %copy-start = (f32[16,1152]{1,0:T(8,128)S(1)}, f32[16,1152]{1,0:T(8,128)}, u32[]{:S(2)}) copy-start(f32[16,1152]{1,0:T(8,128)} %param.18) | copy-start | bytes 221188
  7.2 110.1 %all-reduce.16.cloned.1.call-start = ((), (), s32[]{:S(2)}) async-start(), calls=%async_computation.12 | async-start | bytes 516096
  35.6 3.3 copy-start.10
  38.8 3.1 copy-start.8
  41.9 151.1 %all-gather.16.cloned.1.call-start = ((), (), s32[]{:S(2)}) async-start(), calls=%async_computation | async-start | bytes 4644864 | tf_op jit(solution)/shard_map/all_gather | solution.py:100
  42.0 1.7 copy-start.11
  43.7 5.0 copy-start.12
  43.7 194.1 %all-gather.20.cloned.1.call-start = ((), (), s32[]{:S(2)}) async-start(), calls=%async_computation.6 | async-start | bytes 1658880 | tf_op jit(solution)/shard_map/all_gather | solution.py:107
  44.5 235.6 %all-reduce.8.cloned.1.call-start = ((), (), s32[]{:S(2)}) async-start(), calls=%async_computation.1 | async-start | bytes 2064384 | tf_op jit(solution)/shard_map/psum | solution.py:150
  50.8 142.1 %copy-start.2 = (f32[448,1152]{1,0:T(8,128)}, f32[448,1152]{1,0:T(8,128)S(1)}, u32[]{:S(2)}) copy-start(f32[448,1152]{1,0:T(8,128)S(1)} %get-tuple-element.59) | copy-start | bytes 6193156
  50.8 1.1 copy-start.14
  237.8 3.6 copy-start.6
  241.3 1.8 copy-start.7
  241.3 127.3 %all-gather.22.cloned.1.call-start = ((), (), s32[]{:S(2)}) async-start(), calls=%async_computation.7 | async-start | bytes 5971968 | tf_op jit(solution)/shard_map/all_gather | solution.py:100
  242.6 213.6 %all-gather.24.cloned.1.call-start = ((), (), s32[]{:S(2)}) async-start(), calls=%async_computation.8 | async-start | bytes 5971968 | tf_op jit(solution)/shard_map/all_gather | solution.py:107
  244.3 261.7 %all-reduce.10.cloned.1.call-start = ((), (), s32[]{:S(2)}) async-start(), calls=%async_computation.2 | async-start | bytes 2064384 | tf_op jit(solution)/shard_map/psum | solution.py:160
  467.1 112.7 %all-gather.18.cloned.1.call-start = ((), (), s32[]{:S(2)}) async-start(), calls=%async_computation.3 | async-start | bytes 4644864 | tf_op jit(solution)/shard_map/all_gather | solution.py:100
  468.7 156.0 %all-gather.26.cloned.1.call-start = ((), (), s32[]{:S(2)}) async-start(), calls=%async_computation.9 | async-start | bytes 1658880 | tf_op jit(solution)/shard_map/all_gather | solution.py:107
  469.5 197.7 %all-reduce.12.cloned.1.call-start = ((), (), s32[]{:S(2)}) async-start(), calls=%async_computation.4 | async-start | bytes 2064384 | tf_op jit(solution)/shard_map/psum | solution.py:150
  506.0 1.7 copy-start.5
  628.3 127.5 %all-gather.28.cloned.1.call-start = ((), (), s32[]{:S(2)}) async-start(), calls=%async_computation.10 | async-start | bytes 5971968 | tf_op jit(solution)/shard_map/all_gather | solution.py:100
  629.1 214.3 %all-gather.30.cloned.1.call-start = ((), (), s32[]{:S(2)}) async-start(), calls=%async_computation.11 | async-start | bytes 5971968 | tf_op jit(solution)/shard_map/all_gather | solution.py:107
  629.6 264.3 %all-reduce.14.cloned.1.call-start = ((), (), s32[]{:S(2)}) async-start(), calls=%async_computation.5 | async-start | bytes 2064384 | tf_op jit(solution)/shard_map/psum | solution.py:160
  668.9 1.3 copy-start.3
  843.4 50.6 %copy-start.4 = (f32[1,448,1152]{2,1,0:T(8,128)S(1)}, f32[1,448,1152]{2,1,0:T(8,128)}, u32[]{:S(2)}) copy-start(f32[1,448,1152]{2,1,0:T(8,128)} %copy-done.3) | copy-start | bytes 6193156
  855.0 41.6 %copy-start.13 = (bf16[1152,16]{0,1:T(8,128)(2,1)S(1)}, bf16[1152,16]{0,1:T(8,128)(2,1)}, u32[]{:S(2)}) copy-start(bf16[1152,16]{0,1:T(8,128)(2,1)} %param.25) | copy-start | bytes 110596
  893.9 2.7 copy-start.9
  893.9 8.6 copy-start.1
  897.0 4.8 collective-permute-start
Sparse Core Ops, SparseCore 0:
  42.0 75.2 all-reduce.15
  119.7 73.1 all-gather.15
  195.3 42.4 all-gather.19
  241.5 38.6 all-reduce.7
  282.4 86.2 all-gather.21
  370.9 85.2 all-gather.23
  467.2 38.7 all-reduce.9
  508.4 71.3 all-gather.17
  582.2 42.4 all-gather.25
  628.4 38.6 all-reduce.11
  669.6 86.2 all-gather.27
  758.1 85.2 all-gather.29
  855.2 38.7 all-reduce.13
where the time goes:
time: 917 us; the launch traced here: 909 us
  waiting for transfers between devices  686 us (75%)
  other arithmetic  78.8 us (9%)
  matrix products  68.4 us (7%)
  blocking collectives  32.2 us (4%)
  local copies, waits for them, and re-layouts  23.4 us (3%)
  between operations  19.1 us (2%)
    all_gather x4, waiting for transfers between devices, rows_product(): lax.all_gather(shard, 'batch', axis=0, tiled=True)  248 us
    all_gather x4, waiting for transfers between devices, cols_product(): lax.all_gather(shard, 'batch', axis=1, tiled=True)  224 us
    psum x4, waiting for transfers between devices, local(): branch = lax.psum(branch.astype(jnp.bfloat16), 'tensor').astype(jnp.float32)  147 us
    unnamed x14, waiting for transfers between devices  66.8 us
    slice x1, other arithmetic, local(): hidden_state = hidden_state + modulation[:, 5][:, None, :] * branch  62 us
    dot_general x4, matrix products, cols_product(): jnp.dot(activation, lax.all_gather(shard, 'batch', axis=1, tiled=True), p...  29.7 us
    all_gather x1, blocking collectives, local(): cond_all = lax.all_gather(cond_act, 'batch', axis=0, tiled=True)  25.4 us
  transfers between devices with their start and end apart: 14, of which 13 were waited for; matrix products, arithmetic and copies ran while one was open for 14% of the time, Pallas kernels for 0%

commit v1 on v0

--- a/solution.py
+++ b/solution.py
@@ -157,7 +157,9 @@
         branch = cols_product(hidden_units, down_weight[layer_at]).reshape(
             req_local, max_len, width
         )
-        branch = lax.psum(branch.astype(jnp.bfloat16), "tensor").astype(jnp.float32)
+        branch = jnp.sum(lax.all_gather(branch.astype(jnp.bfloat16), "tensor"), axis=0).astype(
+            jnp.float32
+        )
         hidden_state = hidden_state + modulation[:, 5][:, None, :] * branch
     hidden_state = lax.dynamic_slice_in_dim(hidden_state, own_start, rows_local, 1)
     final_in = modulate(

time: 917 us -> 903 us (0.985)
  waiting for transfers between devices: 686 us -> 666 us
    psum x4 -> x2, waiting for transfers between devices: 147 us -> 72.1 us  [local(): branch = lax.psum(branch.astype(jnp.bfloat16), 'tensor').astype(jnp.float32)]
    all_gather x0 -> x2, waiting for transfers between devices: none -> 56.9 us  [local(): lax.all_gather(branch.astype(jnp.bfloat16), 'tensor')]
  transfers between devices with their start and end apart: 14 -> 14, of which waited for: 13 -> 13; matrix products, arithmetic and copies ran while one was open for 14% -> 15% of each run, Pallas kernels for 0% -> 0%
where the time goes in v1:
time: 903 us; the launch traced here: 896 us
  waiting for transfers between devices  666 us (74%)
  other arithmetic  82.2 us (9%)
  matrix products  67 us (7%)
  blocking collectives  32.2 us (4%)
  local copies, waits for them, and re-layouts  26.8 us (3%)
  between operations  19.3 us (2%)
    all_gather x4, waiting for transfers between devices, rows_product(): lax.all_gather(shard, 'batch', axis=0, tiled=True)  244 us
    all_gather x4, waiting for transfers between devices, cols_product(): lax.all_gather(shard, 'batch', axis=1, tiled=True)  227 us
    psum x2, waiting for transfers between devices, local(): branch = lax.psum(branch.astype(jnp.bfloat16), 'tensor').astype(jnp.float32)  72.1 us
    unnamed x14, waiting for transfers between devices  66.1 us
    slice x1, other arithmetic, local(): hidden_state = hidden_state + modulation[:, 5][:, None, :] * branch  62 us
    all_gather x2, waiting for transfers between devices, local(): lax.all_gather(branch.astype(jnp.bfloat16), 'tensor')  56.9 us
    dot_general x4, matrix products, cols_product(): jnp.dot(activation, lax.all_gather(shard, 'batch', axis=1, tiled=True), p...  29.1 us
    all_gather x1, blocking collectives, local(): cond_all = lax.all_gather(cond_act, 'batch', axis=0, tiled=True)  25.4 us
  transfers between devices with their start and end apart: 14, of which 13 were waited for; matrix products, arithmetic and copies ran while one was open for 15% of the time, Pallas kernels for 0%

profile of v1, /device:TPU:1, one launch (start us, length us, event | category | flops | bytes accessed | tf_op | source)
XLA Modules:
  0.0 895.6 jit_solution(7073533034282829304)
XLA Ops:
  7.9 25.4 %all-gather.8 = bf16[8,1,1152]{2,1,0:T(2,128)(2,1)S(1)} all-gather(bf16[1,1,1152]{2,1,0:T(2,128)(2,1)S(1)} %fusion.114), channel_id=1, replica_groups=mesh['guide'=2,'tensor'=2,'batch'=8] {'batch'}, dimensions={0}, use_global_device_ids=true | all-gather | bytes 20736 | tf_op jit(solution)/shard_map/all_gather | solution.py:112
  33.3 2.2 copy.40
  35.6 3.2 reshape.418
  39.2 2.7 fusion.52
  41.9 0.9 fusion.139
  43.1 1.3 reshape_squeeze.6
  44.5 0.8 fusion.140
  45.4 4.1 multiply_sine_fusion
  49.4 2.1 fusion.141
  53.2 64.1 %all-reduce.10.cloned.1.call-done = f32[8,8064]{1,0:T(8,128)} async-done(((f32[8,8064]{1,0:T(8,128)}), f32[8,8064]{1,0:T(8,128)}) %all-reduce.10.cloned.1.call-update) | async-done | bytes 258064
  117.3 1.7 dynamic-slice_reduce_fusion
  119.2 6.8 all_gather.43
  126.0 62.0 %slice_reduce_fusion.2 = (f32[1152]{0:T(1024)S(1)}, f32[1152]{0:T(1024)S(1)}, f32[1152]{0:T(1024)S(1)}, f32[1152]{0:T(1024)S(1)}, f32[1152]{0:T(1024)S(1)}, /*in...) fusion(f32[1,14,1152]{1,0,2:T(1,128)S(1)} %all_gather.43), kind=kLoop, calls=%fused_computation.104 | loop fusion | flops 5760 | bytes 129024 | tf_op jit(solution)/shard_map/slice | solution.py:163
  188.0 4.9 all-gather.20.cloned.1.call-done
  192.9 5.8 convolution_convert_fusion.1
  198.7 3.9 copy.43
  202.6 7.2 fusion.142
  209.7 4.9 fusion.60
  214.6 23.1 %all-gather.24.cloned.1.call-done = bf16[1,576,1152]{1,2,0:T(8,128)(2,1)} async-done(((bf16[1,576,144]{1,2,0:T(8,128)(2,1)}), bf16[1,576,1152]{1,2,0:T(8,128)(2,1)}) %all-gather.24.cloned.1.call-update) | async-done | bytes 1327120 | tf_op jit(solution)/shard_map/all_gather | solution.py:107
  237.8 3.7 fusion.50
  241.6 1.2 fusion.137
  242.8 2.5 fusion.138
  245.4 34.9 %all-reduce.6.cloned.1.call-done = bf16[1,448,1152]{2,1,0:T(8,128)(2,1)} async-done(((bf16[1,448,1152]{2,1,0:T(8,128)(2,1)}), bf16[1,448,1152]{2,1,0:T(8,128)(2,1)}) %all-reduce.6.cloned.1.call-update) | async-done | bytes 1032208 | tf_op jit(solution)/shard_map/psum | solution.py:150
  280.3 1.7 fusion.132
  282.5 86.3 %all-gather.26.cloned.1.call-done = bf16[1,1152,2304]{2,1,0:T(8,128)(2,1)} async-done(((bf16[1,144,2304]{2,1,0:T(8,128)(2,1)}), bf16[1,1152,2304]{2,1,0:T(8,128)(2,1)}) %all-gather.26.cloned.1.call-update) | async-done | bytes 5308432 | tf_op jit(solution)/shard_map/all_gather | solution.py:100
  368.8 87.5 %all-gather.28.cloned.1.call-done = bf16[1,2304,1152]{1,2,0:T(8,128)(2,1)} async-done(((bf16[1,2304,144]{1,2,0:T(8,128)(2,1)}), bf16[1,2304,1152]{1,2,0:T(8,128)(2,1)}) %all-gather.28.cloned.1.call-update) | async-done | bytes 5308432 | tf_op jit(solution)/shard_map/all_gather | solution.py:107
  456.4 11.1 %fusion.44 = bf16[448,1152]{1,0:T(8,128)(2,1)} fusion(bf16[1,2304,1152]{1,2,0:T(8,128)(2,1)} %all-gather.28.cloned.1.call-done, bf16[1,1152,2304]{2,1,0:T(8,128)(2,1)} %all-gather.26.cloned.1.call-done, f32[1152]{0:T(1024)S(1)} %get-tuple-element.34, f32[1152]{0:T(1024)S(1)} %get-tuple-element.35, f32[448]{0:T(512)S(1)} %add_rsqrt_fusion.2, ...), kind=kOutput, calls=%fused_computation.47 | convolution fusion | flops 4770275328 | bytes 14763008 | tf_op jit(solution)/shard_map/dot_general | solution.py:105
  467.5 2.2 copy.45
  469.8 2.4 reshape_squeeze.7
  473.2 26.3 %all-gather.30.cloned.1.call-done = bf16[896,1152]{1,0:T(8,128)(2,1)} async-done(((bf16[448,1152]{1,0:T(8,128)(2,1)}), bf16[896,1152]{1,0:T(8,128)(2,1)}) %all-gather.30.cloned.1.call-update) | async-done | bytes 2064400 | tf_op jit(solution)/shard_map/all_gather | solution.py:160
  499.4 3.2 reduce.20
  502.6 1.8 fusion.135
  504.5 1.3 copy-done.2
  506.1 67.2 %all-gather.22.cloned.1.call-done = bf16[1152,1728]{1,0:T(8,128)(2,1)} async-done(((bf16[144,1728]{1,0:T(8,128)(2,1)}), bf16[1152,1728]{1,0:T(8,128)(2,1)}) %all-gather.22.cloned.1.call-update) | async-done | bytes 3981328 | tf_op jit(solution)/shard_map/all_gather | solution.py:100
  573.3 5.1 convolution_convert_fusion
  578.4 1.4 copy.46
  579.8 5.9 fusion.143
  585.8 3.9 fusion.59
  589.7 28.5 %all-gather.32.cloned.1.call-done = bf16[1,576,1152]{1,2,0:T(8,128)(2,1)} async-done(((bf16[1,576,144]{1,2,0:T(8,128)(2,1)}), bf16[1,576,1152]{1,2,0:T(8,128)(2,1)}) %all-gather.32.cloned.1.call-update) | async-done | bytes 1327120 | tf_op jit(solution)/shard_map/all_gather | solution.py:107
  618.1 3.4 fusion.51
  623.2 37.2 %all-reduce.8.cloned.1.call-done = bf16[1,448,1152]{2,1,0:T(8,128)(2,1)} async-done(((bf16[1,448,1152]{2,1,0:T(8,128)(2,1)}), bf16[1,448,1152]{2,1,0:T(8,128)(2,1)}) %all-reduce.8.cloned.1.call-update) | async-done | bytes 1032208 | tf_op jit(solution)/shard_map/psum | solution.py:150
  660.4 2.2 fusion.134
  663.0 86.1 %all-gather.34.cloned.1.call-done = bf16[1,1152,2304]{2,1,0:T(8,128)(2,1)} async-done(((bf16[1,144,2304]{2,1,0:T(8,128)(2,1)}), bf16[1,1152,2304]{2,1,0:T(8,128)(2,1)}) %all-gather.34.cloned.1.call-update) | async-done | bytes 5308432 | tf_op jit(solution)/shard_map/all_gather | solution.py:100
  749.1 87.5 %all-gather.36.cloned.1.call-done = bf16[1,2304,1152]{1,2,0:T(8,128)(2,1)} async-done(((bf16[1,2304,144]{1,2,0:T(8,128)(2,1)}), bf16[1,2304,1152]{1,2,0:T(8,128)(2,1)}) %all-gather.36.cloned.1.call-update) | async-done | bytes 5308432 | tf_op jit(solution)/shard_map/all_gather | solution.py:107
  836.6 10.9 %fusion.47 = bf16[448,1152]{1,0:T(8,128)(2,1)} fusion(bf16[1,2304,1152]{1,2,0:T(8,128)(2,1)} %all-gather.36.cloned.1.call-done, bf16[1,1152,2304]{2,1,0:T(8,128)(2,1)} %all-gather.34.cloned.1.call-done, f32[1,448,1152]{2,1,0:T(8,128)S(1)} %get-tuple-element.45, f32[1152]{0:T(1024)S(1)} %get-tuple-element.25, f32[1152]{0:T(1024)S(1)} %get-tuple-element.26, ...), kind=kOutput, calls=%fused_computation.48 | convolution fusion | flops 4768727040 | bytes 13726208 | tf_op jit(solution)/shard_map/dot_general | solution.py:105
  848.9 30.6 %all-gather.38.cloned.1.call-done = bf16[896,1152]{1,0:T(8,128)(2,1)} async-done(((bf16[448,1152]{1,0:T(8,128)(2,1)}), bf16[896,1152]{1,0:T(8,128)(2,1)}) %all-gather.38.cloned.1.call-update) | async-done | bytes 2064400 | tf_op jit(solution)/shard_map/all_gather | solution.py:160
  879.5 2.5 reduce.21
  883.1 0.8 collective-permute-start
  (87 shorter events, 10.1 us)
Async XLA Ops:
  7.2 42.3 %copy-start = (f32[16,1152]{1,0:T(8,128)S(1)}, f32[16,1152]{1,0:T(8,128)}, u32[]{:S(2)}) copy-start(f32[16,1152]{1,0:T(8,128)} %param.18) | copy-start | bytes 221188
  7.2 110.1 %all-reduce.10.cloned.1.call-start = ((), (), s32[]{:S(2)}) async-start(), calls=%async_computation.12 | async-start | bytes 516096
  35.6 3.3 copy-start.6
  38.8 3.1 copy-start.5
  41.9 151.1 %all-gather.20.cloned.1.call-start = ((), (), s32[]{:S(2)}) async-start(), calls=%async_computation | async-start | bytes 4644864 | tf_op jit(solution)/shard_map/all_gather | solution.py:100
  42.8 1.7 copy-start.7
  44.4 5.0 copy-start.8
  44.4 193.3 %all-gather.24.cloned.1.call-start = ((), (), s32[]{:S(2)}) async-start(), calls=%async_computation.4 | async-start | bytes 1658880 | tf_op jit(solution)/shard_map/all_gather | solution.py:107
  45.3 235.0 %all-reduce.6.cloned.1.call-start = ((), (), s32[]{:S(2)}) async-start(), calls=%async_computation.1 | async-start | bytes 2064384 | tf_op jit(solution)/shard_map/psum | solution.py:150
  51.5 1.1 copy-start.10
  237.8 3.8 copy-start.4
  241.5 127.3 %all-gather.26.cloned.1.call-start = ((), (), s32[]{:S(2)}) async-start(), calls=%async_computation.5 | async-start | bytes 5971968 | tf_op jit(solution)/shard_map/all_gather | solution.py:100
  242.8 213.6 %all-gather.28.cloned.1.call-start = ((), (), s32[]{:S(2)}) async-start(), calls=%async_computation.6 | async-start | bytes 5971968 | tf_op jit(solution)/shard_map/all_gather | solution.py:107
  245.3 254.1 %all-gather.30.cloned.1.call-start = ((), (), s32[]{:S(2)}) async-start(), calls=%async_computation.7 | async-start | bytes 3096576 | tf_op jit(solution)/shard_map/all_gather | solution.py:160
  280.3 1.7 copy-start.3
  467.5 105.8 %all-gather.22.cloned.1.call-start = ((), (), s32[]{:S(2)}) async-start(), calls=%async_computation.2 | async-start | bytes 4644864 | tf_op jit(solution)/shard_map/all_gather | solution.py:100
  472.2 146.0 %all-gather.32.cloned.1.call-start = ((), (), s32[]{:S(2)}) async-start(), calls=%async_computation.8 | async-start | bytes 1658880 | tf_op jit(solution)/shard_map/all_gather | solution.py:107
  472.9 187.5 %all-reduce.8.cloned.1.call-start = ((), (), s32[]{:S(2)}) async-start(), calls=%async_computation.3 | async-start | bytes 2064384 | tf_op jit(solution)/shard_map/psum | solution.py:150
  504.4 1.3 copy-start.2
  621.6 127.5 %all-gather.34.cloned.1.call-start = ((), (), s32[]{:S(2)}) async-start(), calls=%async_computation.9 | async-start | bytes 5971968 | tf_op jit(solution)/shard_map/all_gather | solution.py:100
  622.3 214.3 %all-gather.36.cloned.1.call-start = ((), (), s32[]{:S(2)}) async-start(), calls=%async_computation.10 | async-start | bytes 5971968 | tf_op jit(solution)/shard_map/all_gather | solution.py:107
  622.9 256.6 %all-gather.38.cloned.1.call-start = ((), (), s32[]{:S(2)}) async-start(), calls=%async_computation.11 | async-start | bytes 3096576 | tf_op jit(solution)/shard_map/all_gather | solution.py:160
  882.0 0.8 copy-start.9
  882.0 6.6 copy-start.1
  883.1 4.8 collective-permute-start
Sparse Core Ops, SparseCore 0:
  42.0 75.2 all-reduce.9
  119.7 73.1 all-gather.19
  195.3 42.4 all-gather.23
  241.6 38.6 all-reduce.5
  282.6 86.2 all-gather.25
  371.1 85.2 all-gather.27
  467.6 31.7 all-gather.29
  501.9 71.3 all-gather.21
  575.7 42.4 all-gather.31
  621.7 38.6 all-reduce.7
  662.8 86.2 all-gather.33
  751.3 85.2 all-gather.35
  847.7 31.7 all-gather.37
